TPU v7x, 32 devices: a whole 2x2x4 slice. The times are simulated.
32 devices in a mesh: dp: 4 (over y, x), tile: 8 (over z, core).
Axes of the slice: x: 2, y: 2, z: 4, core: 2. Of those that a mesh axis runs over, the one named last changes fastest.
Arguments:
- tokens: bfloat16 [512, 4096], P('dp', 'tile'), may hold values from -6 to 6
- grad_out: bfloat16 [512, 4096], P('dp', 'tile'), may hold values from -6 to 6
- up_tiles: bfloat16 [8, 256, 128, 128], P('tile'), may hold values from -0.1875 to 0.1875
- down_tiles: bfloat16 [8, 256, 128, 128], P('tile'), may hold values from -0.09375 to 0.09375
- tile_rows: int32 [8, 256], P('tile'), may hold values from 0 to 15, as said below
- tile_cols: int32 [8, 256], P('tile'), may hold values from 0 to 31
- tile_count: int32 [8], P('tile'), may hold values from 32 to 256, as said below
Outputs:
- mixed: bfloat16 [512, 4096], P('dp', 'tile')
- grad_in: bfloat16 [512, 4096], P('dp', 'tile')
- grad_up: float32 [8, 256, 128, 128], P('tile', 'dp')
- grad_down: float32 [8, 256, 128, 128], P('tile', 'dp')
Inputs may be any that keep to these rules, and one draw needn't show every extreme that they name: `tile_count`: some owner holds exactly 256 tiles in every draw. The pairs (tile_rows[i, s], tile_cols[i, s]) of one owner are distinct over all its 256 slots.
All inputs are finite; a program needn't handle non-finite values.
Results may differ from a plain program's by a relative error of at most 0.015.
Values may be sent and summed in bfloat16 or wider, within the bound.
A program may use at most 192 MiB of HBM per device.

v0:
```python
import jax
import jax.numpy as jnp
from jax import lax
from jax.sharding import PartitionSpec as P

HIDDEN_SIZE = 16384


def gelu_pair(pre):
    curve = jax.scipy.special.erf(pre * 0.7071067811865476)
    value = 0.5 * pre * (1.0 + curve)
    slope = 0.5 * (1.0 + curve) + pre * jnp.exp(-0.5 * pre * pre) * 0.3989422804014327
    return (value, slope)


def body(tokens, grad_out, up_tiles, down_tiles, tile_rows, tile_cols, tile_count):
    side = up_tiles.shape[2]
    slots = up_tiles.shape[1]
    rows = tile_rows[0]
    cols = tile_cols[0]
    valid = jnp.arange(slots, dtype=jnp.int32) < tile_count[0]
    keep = valid.astype(jnp.bfloat16)
    live = valid.astype(jnp.float32)[:, None, None]
    up_live = up_tiles[0] * keep[:, None, None]
    down_live = down_tiles[0] * keep[:, None, None]
    row_blocks = HIDDEN_SIZE // (side * lax.axis_size("tile"))
    whole_in, whole_grad = (
        lax.all_gather(tokens, "tile", axis=1, tiled=True),
        lax.all_gather(grad_out, "tile", axis=1, tiled=True),
    )
    count_tok = whole_in.shape[0]
    width = whole_in.shape[1]
    blocks = width // side
    row_onehot = (rows[:, None] == jnp.arange(row_blocks, dtype=jnp.int32)[None, :]).astype(
        jnp.float32
    )
    col_onehot = (cols[:, None] == jnp.arange(blocks, dtype=jnp.int32)[None, :]).astype(jnp.float32)
    highest = lax.Precision.HIGHEST
    x_slots = whole_in.reshape(count_tok, blocks, side)[:, cols]
    dy_slots = whole_grad.reshape(count_tok, blocks, side)[:, cols]
    pre_slots = jnp.einsum("tsk,skj->tsj", x_slots, up_live, preferred_element_type=jnp.float32)
    pre = jnp.einsum("tsj,sr->trj", pre_slots, row_onehot, precision=highest)
    value, slope = gelu_pair(pre)
    hidden = value.astype(jnp.bfloat16)
    h_slots = hidden[:, rows]
    out_slots = jnp.einsum("tsj,sjk->tsk", h_slots, down_live, preferred_element_type=jnp.float32)
    out_part = jnp.einsum("tsk,sc->tck", out_slots, col_onehot, precision=highest).reshape(
        count_tok, width
    )
    out_term = out_part.astype(jnp.bfloat16).astype(jnp.float32)
    mixed = lax.psum_scatter(out_term.astype(jnp.bfloat16), "tile", scatter_dimension=1, tiled=True)
    scale = 1.0 / lax.axis_size("dp")
    down_term = (
        (jnp.einsum("tsj,tsk->sjk", h_slots, dy_slots, preferred_element_type=jnp.float32) * live)
        .astype(jnp.bfloat16)
        .astype(jnp.float32)
    )
    hid_slots = jnp.einsum("tsk,sjk->tsj", dy_slots, down_live, preferred_element_type=jnp.float32)
    grad_hidden = jnp.einsum("tsj,sr->trj", hid_slots, row_onehot, precision=highest)
    grad_pre = (grad_hidden * slope).astype(jnp.bfloat16)
    pre_grad_slots = grad_pre[:, rows]
    in_slots = jnp.einsum(
        "tsj,skj->tsk", pre_grad_slots, up_live, preferred_element_type=jnp.float32
    )
    in_part = jnp.einsum("tsk,sc->tck", in_slots, col_onehot, precision=highest).reshape(
        count_tok, width
    )
    in_term = in_part.astype(jnp.bfloat16).astype(jnp.float32)
    up_term = (
        (
            jnp.einsum("tsk,tsj->skj", x_slots, pre_grad_slots, preferred_element_type=jnp.float32)
            * live
        )
        .astype(jnp.bfloat16)
        .astype(jnp.float32)
    )
    down_total, up_total = (
        lax.psum_scatter(
            down_term.astype(jnp.bfloat16), "dp", scatter_dimension=0, tiled=True
        ).astype(jnp.float32),
        lax.psum_scatter(
            up_term.astype(jnp.bfloat16), "dp", scatter_dimension=0, tiled=True
        ).astype(jnp.float32),
    )
    grad_down = down_total * scale
    grad_up = up_total * scale
    grad_in = lax.psum_scatter(
        in_term.astype(jnp.bfloat16), "tile", scatter_dimension=1, tiled=True
    )
    return (mixed, grad_in, grad_up[None], grad_down[None])


def solution(mesh):
    placed = (
        P("dp", "tile"),
        P("dp", "tile"),
        P("tile", None, None, None),
        P("tile", None, None, None),
        P("tile", None),
        P("tile", None),
        P("tile"),
    )
    return jax.shard_map(
        body,
        mesh=mesh,
        in_specs=placed,
        out_specs=(
            P("dp", "tile"),
            P("dp", "tile"),
            P("tile", "dp", None, None),
            P("tile", "dp", None, None),
        ),
        check_vma=False,
    )
```

profile of v0, /device:TPU:0, one launch (start us, length us, event | category | flops | bytes accessed | tf_op | source)
XLA Modules:
  0.0 398.8 jit_solution(1062021580892563932)
XLA Ops:
  7.2 0.0 all-gather.3.cloned.1.call-start
  7.2 1.7 copy.17
  8.9 0.0 all-gather.3.cloned.1.call-update
  8.9 0.0 all-gather.5.cloned.1.call-start
  8.9 1.7 copy.24
  10.6 0.0 all-gather.5.cloned.1.call-update
  10.6 0.0 reduce-scatter.11.cloned.1.call-start
  11.3 0.7 compare_select_fusion.1
  12.0 0.7 compare_select_fusion
  12.7 22.4 %all-gather.3.cloned.1.call-done = bf16[128,4096]{0,1:T(8,128)(2,1)} async-done(((bf16[128,512]{0,1:T(8,128)(2,1)}), bf16[128,4096]{0,1:T(8,128)(2,1)}) %all-gather.3.cloned.1.call-update) | async-done | bytes 1048592 | tf_op jit(solution)/shard_map/all_gather | solution.py:28
  35.1 1.6 copy.18
  36.8 22.4 %all-gather.5.cloned.1.call-done = bf16[128,4096]{0,1:T(8,128)(2,1)} async-done(((bf16[128,512]{0,1:T(8,128)(2,1)}), bf16[128,4096]{0,1:T(8,128)(2,1)}) %all-gather.5.cloned.1.call-update) | async-done | bytes 1048592 | tf_op jit(solution)/shard_map/all_gather | solution.py:29
  59.2 1.6 copy.25
  60.8 8.6 %gather_fusion.2 = bf16[256,128,128]{2,1,0:T(8,128)(2,1)} fusion(bf16[128,32,128]{2,0,1:T(8,128)(2,1)S(1)} %copy.25, s32[1024]{0:T(1024)S(1)} %pad_clamp_fusion.1), kind=kCustom, calls=%fused_computation.2 | custom fusion | bytes 16778240 | tf_op jit(solution)/shard_map/gather | solution.py:40
  69.4 8.6 %gather_fusion = bf16[256,128,128]{2,1,0:T(8,128)(2,1)} fusion(bf16[128,32,128]{2,0,1:T(8,128)(2,1)S(1)} %copy.18, s32[1024]{0:T(1024)S(1)} %pad_clamp_fusion.1), kind=kCustom, calls=%fused_computation | custom fusion | bytes 16778240 | tf_op jit(solution)/shard_map/gather | solution.py:39
  78.0 13.1 %convolution_bitcast_fusion.3 = f32[128,256,128]{0,2,1:T(8,128)} fusion(bf16[256,128,128]{2,1,0:T(8,128)(2,1)} %gather_fusion, bf16[1,256,128,128]{3,2,1,0:T(8,128)(2,1)} %param.9, bf16[256]{0:T(256)(128)(2,1)S(1)} %get-tuple-element.7), kind=kOutput, calls=%fused_computation.9 | convolution fusion | flops 1077936128 | bytes 33554944 | tf_op jit(solution)/shard_map/tsk,skj->tsj/dot_general | solution.py:41
  91.1 17.5 %copy.20 = f32[128,256,128]{2,1,0:T(8,128)} copy(f32[128,256,128]{0,2,1:T(8,128)} %convolution_bitcast_fusion.3) | data formatting | bytes 33554432 | tf_op jit(solution)/shard_map/tsk,skj->tsj/transpose | solution.py:41
  108.6 9.1 %multiply_convert_fusion.2 = (bf16[128,16,128]{2,1,0:T(8,128)(2,1)S(1)}, f32[128,16,128]{2,1,0:T(8,128)S(1)}) fusion(f32[128,256,128]{2,1,0:T(8,128)} %copy.20, s32[256]{0:T(256)S(1)} %bitcast.90), kind=kOutput, calls=%fused_computation.39 | convolution fusion | flops 806621184 | bytes 18351104 | tf_op jit(solution)/shard_map/tsj,sr->trj/dot_general | solution.py:42
  117.7 0.1 copy.21
  117.9 19.4 %gather_fusion.1 = bf16[256,128,128]{2,1,0:T(8,128)(2,1)} fusion(bf16[128,16,128]{2,0,1:T(8,128)(2,1)S(1)} %copy.21, s32[1024]{0:T(1024)S(1)} %pad_clamp_fusion), kind=kCustom, calls=%fused_computation.1 | custom fusion | bytes 16778240 | tf_op jit(solution)/shard_map/gather | solution.py:45
  137.3 10.0 %multiply_convert_fusion = bf16[256,128,128]{2,1,0:T(8,128)(2,1)} fusion(bf16[256,128,128]{2,1,0:T(8,128)(2,1)} %gather_fusion.2, bf16[256,128,128]{2,1,0:T(8,128)(2,1)} %gather_fusion.1, f32[256]{0:T(256)S(1)} %get-tuple-element.6), kind=kOutput, calls=%fused_computation.4 | convolution fusion | flops 1082130432 | bytes 25166848 | tf_op jit(solution)/shard_map/tsj,tsk->sjk/dot_general | solution.py:54
  147.2 0.0 reduce-scatter.11.cloned.1.call-update
  147.3 0.0 reduce-scatter.9.cloned.1.call-start
  147.3 12.8 %convolution_bitcast_fusion.1 = f32[128,256,128]{0,2,1:T(8,128)} fusion(bf16[256,128,128]{2,1,0:T(8,128)(2,1)} %gather_fusion.2, bf16[1,256,128,128]{3,2,1,0:T(8,128)(2,1)} %param.10, bf16[256]{0:T(256)(128)(2,1)S(1)} %get-tuple-element.7), kind=kOutput, calls=%fused_computation.7 | convolution fusion | flops 1077936128 | bytes 33554944 | tf_op jit(solution)/shard_map/tsk,sjk->tsj/dot_general | solution.py:58
  160.1 17.7 %copy.26 = f32[128,256,128]{2,1,0:T(8,128)} copy(f32[128,256,128]{0,2,1:T(8,128)} %convolution_bitcast_fusion.1) | data formatting | bytes 33554432 | tf_op jit(solution)/shard_map/tsk,sjk->tsj/transpose | solution.py:58
  177.8 9.5 %fusion.13 = bf16[128,16,128]{2,1,0:T(8,128)(2,1)S(1)} fusion(f32[128,256,128]{2,1,0:T(8,128)} %copy.26, f32[128,16,128]{2,1,0:T(8,128)S(1)} %get-tuple-element.5, s32[256]{0:T(256)S(1)} %bitcast.91), kind=kOutput, calls=%fused_computation.32 | convolution fusion | flops 807931904 | bytes 18351104 | tf_op jit(solution)/shard_map/tsj,sr->trj/dot_general | solution.py:59
  187.3 0.1 copy.27
  187.5 8.6 %gather_fusion.3 = bf16[256,128,128]{2,1,0:T(8,128)(2,1)} fusion(bf16[128,16,128]{2,0,1:T(8,128)(2,1)S(1)} %copy.27, s32[1024]{0:T(1024)S(1)} %pad_clamp_fusion), kind=kCustom, calls=%fused_computation.3 | custom fusion | bytes 16778240 | tf_op jit(solution)/shard_map/gather | solution.py:61
  196.1 10.1 %multiply_convert_fusion.1 = bf16[256,128,128]{2,1,0:T(8,128)(2,1)} fusion(bf16[256,128,128]{2,1,0:T(8,128)(2,1)} %gather_fusion.3, bf16[256,128,128]{2,1,0:T(8,128)(2,1)} %gather_fusion, f32[256]{0:T(256)S(1)} %get-tuple-element.6), kind=kOutput, calls=%fused_computation.5 | convolution fusion | flops 1082130432 | bytes 25166848 | tf_op jit(solution)/shard_map/tsk,tsj->skj/dot_general | solution.py:71
  206.1 0.0 reduce-scatter.9.cloned.1.call-update
  206.2 0.0 reduce-scatter.5.cloned.1.call-start
  206.2 13.9 %convolution_bitcast_fusion.2 = f32[128,256,128]{0,2,1:T(8,128)} fusion(bf16[256,128,128]{2,1,0:T(8,128)(2,1)} %gather_fusion.1, bf16[1,256,128,128]{3,2,1,0:T(8,128)(2,1)} %param.10, bf16[256]{0:T(256)(128)(2,1)S(1)} %get-tuple-element.7), kind=kOutput, calls=%fused_computation.8 | convolution fusion | flops 1077936128 | bytes 33554944 | tf_op jit(solution)/shard_map/tsj,sjk->tsk/dot_general | solution.py:46
  220.1 17.6 %copy.23 = f32[128,256,128]{2,1,0:T(8,128)} copy(f32[128,256,128]{0,2,1:T(8,128)} %convolution_bitcast_fusion.2) | data formatting | bytes 33554432 | tf_op jit(solution)/shard_map/tsj,sjk->tsk/transpose | solution.py:46
  237.7 9.8 %convolution_convert_fusion.1 = bf16[32,128,128]{2,0,1:T(8,128)(2,1)S(1)} fusion(f32[128,256,128]{2,1,0:T(8,128)} %copy.23, s32[256]{0:T(256)S(1)} %bitcast.92), kind=kOutput, calls=%fused_computation.28 | convolution fusion | flops 1611145216 | bytes 17826816 | tf_op jit(solution)/shard_map/tsk,sc->tck/dot_general | solution.py:47
  247.5 1.4 copy.40
  248.9 0.0 reduce-scatter.5.cloned.1.call-update
  248.9 0.0 reduce-scatter.7.cloned.1.call-start
  249.0 13.3 %convolution_bitcast_fusion = f32[128,256,128]{0,2,1:T(8,128)} fusion(bf16[256,128,128]{2,1,0:T(8,128)(2,1)} %gather_fusion.3, bf16[1,256,128,128]{3,2,1,0:T(8,128)(2,1)} %param.9, bf16[256]{0:T(256)(128)(2,1)S(1)} %get-tuple-element.7), kind=kOutput, calls=%fused_computation.6 | convolution fusion | flops 1077936128 | bytes 33554944 | tf_op jit(solution)/shard_map/tsj,skj->tsk/dot_general | solution.py:62
  262.2 18.0 %copy.28 = f32[128,256,128]{2,1,0:T(8,128)} copy(f32[128,256,128]{0,2,1:T(8,128)} %convolution_bitcast_fusion) | data formatting | bytes 33554432 | tf_op jit(solution)/shard_map/tsj,skj->tsk/transpose | solution.py:62
  280.3 9.9 %convolution_convert_fusion = bf16[32,128,128]{2,0,1:T(8,128)(2,1)S(1)} fusion(f32[128,256,128]{2,1,0:T(8,128)} %copy.28, s32[256]{0:T(256)S(1)} %bitcast.93), kind=kOutput, calls=%fused_computation.27 | convolution fusion | flops 1611145216 | bytes 17826816 | tf_op jit(solution)/shard_map/tsk,sc->tck/dot_general | solution.py:65
  290.1 1.5 copy.39
  291.6 0.0 reduce-scatter.7.cloned.1.call-update
  291.6 0.0 reduce-scatter.11.cloned.1.call-done
  291.7 4.2 %multiply_bitcast_fusion = f32[1,64,128,128]{3,2,1,0:T(8,128)} fusion(bf16[64,128,128]{2,1,0:T(8,128)(2,1)} %reduce-scatter.11.cloned.1.call-done), kind=kLoop, calls=%fused_computation.20 | loop fusion | flops 2097152 | bytes 6291456 | tf_op jit(solution)/shard_map/broadcast_in_dim | solution.py:90
  295.8 26.8 %reduce-scatter.9.cloned.1.call-done = bf16[64,128,128]{2,1,0:T(8,128)(2,1)} async-done(((bf16[256,128,128]{2,1,0:T(8,128)(2,1)}), bf16[64,128,128]{2,1,0:T(8,128)(2,1)}) %reduce-scatter.9.cloned.1.call-update) | async-done | bytes 2097168 | tf_op jit(solution)/shard_map/reduce_scatter | solution.py:81
  322.6 4.2 %multiply_bitcast_fusion.1 = f32[1,64,128,128]{3,2,1,0:T(8,128)} fusion(bf16[64,128,128]{2,1,0:T(8,128)(2,1)} %reduce-scatter.9.cloned.1.call-done), kind=kLoop, calls=%fused_computation.21 | loop fusion | flops 2097152 | bytes 6291456 | tf_op jit(solution)/shard_map/broadcast_in_dim | solution.py:90
  326.8 31.2 %reduce-scatter.5.cloned.1.call-done = bf16[128,512]{1,0:T(8,128)(2,1)} async-done(((bf16[128,4096]{1,0:T(8,128)(2,1)}), bf16[128,512]{1,0:T(8,128)(2,1)}) %reduce-scatter.5.cloned.1.call-update) | async-done | bytes 131088 | tf_op jit(solution)/shard_map/reduce_scatter | solution.py:51
  358.0 33.6 %reduce-scatter.7.cloned.1.call-done = bf16[128,512]{1,0:T(8,128)(2,1)} async-done(((bf16[128,4096]{1,0:T(8,128)(2,1)}), bf16[128,512]{1,0:T(8,128)(2,1)}) %reduce-scatter.7.cloned.1.call-update) | async-done | bytes 131088 | tf_op jit(solution)/shard_map/reduce_scatter | solution.py:87
  (7 shorter events, 0.0 us)
Async XLA Ops:
  7.2 28.0 %all-gather.3.cloned.1.call-start = ((), (), s32[]{:S(2)}) async-start(), calls=%async_computation.4 | async-start | bytes 1179648 | tf_op jit(solution)/shard_map/all_gather | solution.py:28
  8.9 50.3 %all-gather.5.cloned.1.call-start = ((), (), s32[]{:S(2)}) async-start(), calls=%async_computation.6 | async-start | bytes 1179648 | tf_op jit(solution)/shard_map/all_gather | solution.py:29
  10.6 281.0 %reduce-scatter.11.cloned.1.call-start = ((), (), s32[]{:S(2)}) async-start(), calls=%async_computation.9 | async-start | bytes 10485760 | tf_op jit(solution)/shard_map/reduce_scatter | solution.py:78
  91.1 17.5 %copy-start = (s32[1,256]{1,0:T(1,128)S(1)}, s32[1,256]{1,0:T(1,128)}, u32[]{:S(2)}) copy-start(s32[1,256]{1,0:T(1,128)} %param.11) | copy-start | bytes 3076
  147.3 175.4 %reduce-scatter.9.cloned.1.call-start = ((), (), s32[]{:S(2)}) async-start(), calls=%async_computation.8 | async-start | bytes 10485760 | tf_op jit(solution)/shard_map/reduce_scatter | solution.py:81
  206.2 151.8 %reduce-scatter.5.cloned.1.call-start = ((), (), s32[]{:S(2)}) async-start(), calls=%async_computation.5 | async-start | bytes 1179648 | tf_op jit(solution)/shard_map/reduce_scatter | solution.py:51
  220.1 17.6 %copy-start.1 = (s32[1,256]{1,0:T(1,128)S(1)}, s32[1,256]{1,0:T(1,128)}, u32[]{:S(2)}) copy-start(s32[1,256]{1,0:T(1,128)} %param.12) | copy-start | bytes 3076
  248.9 142.6 %reduce-scatter.7.cloned.1.call-start = ((), (), s32[]{:S(2)}) async-start(), calls=%async_computation.7 | async-start | bytes 1179648 | tf_op jit(solution)/shard_map/reduce_scatter | solution.py:87
Sparse Core Ops, SparseCore 0:
  10.1 24.9 all-gather.2
  37.3 21.8 all-gather.4
  147.4 85.9 reduce-scatter.10
  236.3 86.3 reduce-scatter.8
  325.3 32.6 reduce-scatter.4
  360.7 30.8 reduce-scatter.6
where the time goes:
time: 403 us; the launch traced here: 399 us
  waiting for transfers between devices  136 us (34%)
  local copies, waits for them, and re-layouts  126 us (31%)
  matrix products  111 us (28%)
  between operations  15.3 us (4%)
  other arithmetic  9.71 us (2%)
    reduce_scatter x1, waiting for transfers between devices, body(): lax.psum_scatter(in_term.astype(jnp.bfloat16), 'tile', scatter_dimension=...  33.6 us
    reduce_scatter x1, waiting for transfers between devices, body(): lax.psum_scatter(out_term.astype(jnp.bfloat16), 'tile', scatter_dimension...  31.2 us
    reduce_scatter x1, waiting for transfers between devices, body(): lax.psum_scatter(up_term.astype(jnp.bfloat16), 'dp', scatter_dimension=0,...  26.8 us
    all_gather x1, waiting for transfers between devices, body(): lax.all_gather(grad_out, 'tile', axis=1, tiled=True)  22.4 us
    all_gather x1, waiting for transfers between devices, body(): lax.all_gather(tokens, 'tile', axis=1, tiled=True)  22.4 us
    gather x1, local copies, waits for them, and re-layouts, body(): h_slots = hidden[:, rows]  19.4 us
    transpose x1, local copies, waits for them, and re-layouts, body(): jnp.einsum('tsj,skj->tsk', pre_grad_slots, up_live, preferred_element_typ...  18 us
    transpose x1, local copies, waits for them, and re-layouts, body(): jnp.einsum('tsk,sjk->tsj', dy_slots, down_live, preferred_element_type=jn...  17.7 us
  transfers between devices with their start and end apart: 6, of which 5 were waited for; matrix products, arithmetic and copies ran while one was open for 39% of the time, Pallas kernels for 0%

commit v1 on v0

v1 whole, which is shorter than its diff:
```python
import functools

import jax
import jax.numpy as jnp
from jax import lax
from jax.experimental import pallas as pl
from jax.experimental.pallas import tpu as pltpu
from jax.sharding import PartitionSpec as P

HIDDEN_SIZE = 16384
VMEM_LIMIT = 64 * 1024 * 1024 - 65536


def gelu_pair(pre):
    curve = lax.erf(pre * 0.7071067811865476)
    value = 0.5 * pre * (1.0 + curve)
    slope = 0.5 * (1.0 + curve) + pre * jnp.exp(-0.5 * pre * pre) * 0.3989422804014327
    return (value, slope)


def dense_kernel(rows, cols, count, up, down, up_out, down_out, up_buf, down_buf, sems, out_sems):
    side = up.shape[1]
    live = count[0]

    def clear(buf):
        step = 16

        @pl.loop(0, buf.shape[0] // step)
        def _(i):
            buf[pl.ds(pl.multiple_of(i * step, step), step), :] = jnp.zeros((step, buf.shape[1]), buf.dtype)

    def up_copy(s):
        r = pl.multiple_of(rows[s] * side, side)
        c = pl.multiple_of(cols[s] * side, side)
        return pltpu.make_async_copy(up.at[s], up_buf.at[pl.ds(c, side), pl.ds(r, side)], sems.at[0])

    def down_copy(s):
        r = pl.multiple_of(rows[s] * side, side)
        c = pl.multiple_of(cols[s] * side, side)
        return pltpu.make_async_copy(down.at[s], down_buf.at[pl.ds(r, side), pl.ds(c, side)], sems.at[1])

    clear(up_buf)

    @pl.loop(0, live)
    def _(s):
        up_copy(s).start()

    clear(down_buf)

    @pl.loop(0, live)
    def _(s):
        down_copy(s).start()

    @pl.loop(0, live)
    def _(s):
        up_copy(s).wait()

    first = pltpu.make_async_copy(up_buf, up_out, out_sems.at[0])
    first.start()

    @pl.loop(0, live)
    def _(s):
        down_copy(s).wait()

    second = pltpu.make_async_copy(down_buf, down_out, out_sems.at[1])
    second.start()
    first.wait()
    second.wait()


def densify(rows, cols, count, up, down, width, hidden):
    smem = pl.BlockSpec(memory_space=pltpu.SMEM)
    hbm = pl.BlockSpec(memory_space=pl.ANY)
    return pl.pallas_call(
        dense_kernel,
        out_shape=(
            jax.ShapeDtypeStruct((width, hidden), up.dtype),
            jax.ShapeDtypeStruct((hidden, width), up.dtype),
        ),
        in_specs=[smem, smem, smem, hbm, hbm],
        out_specs=(hbm, hbm),
        scratch_shapes=[
            pltpu.VMEM((width, hidden), up.dtype),
            pltpu.VMEM((hidden, width), up.dtype),
            pltpu.SemaphoreType.DMA((2,)),
            pltpu.SemaphoreType.DMA((2,)),
        ],
        compiler_params=pltpu.CompilerParams(vmem_limit_bytes=VMEM_LIMIT),
        cost_estimate=pl.CostEstimate(flops=0, bytes_accessed=6 * width * hidden, transcendentals=0),
        name="densify",
    )(rows, cols, count, up, down)


NT = (((1,), (1,)), ((), ()))
TN = (((0,), (0,)), ((), ()))


def layer_kernel(x, up, down, hg, part, out_acc, in_acc):
    step = pl.program_id(0)
    owners, _, _, feats = x.shape

    @pl.when(step == 0)
    def _():
        out_acc[...] = jnp.zeros_like(out_acc)
        in_acc[...] = jnp.zeros_like(in_acc)

    pre = jnp.zeros(hg.shape[1:], jnp.float32)
    grad_hidden = jnp.zeros(hg.shape[1:], jnp.float32)
    for t in range(owners):
        span = slice(t * feats, (t + 1) * feats)
        pre += jnp.dot(x[t, 0], up[span, :], preferred_element_type=jnp.float32)
        grad_hidden += lax.dot_general(x[t, 1], down[:, span], NT, preferred_element_type=jnp.float32)
    value, slope = gelu_pair(pre)
    hidden = value.astype(jnp.bfloat16)
    grad_pre = (grad_hidden * slope).astype(jnp.bfloat16)
    hg[0] = hidden
    hg[1] = grad_pre
    for t in range(owners):
        span = slice(t * feats, (t + 1) * feats)
        out_acc[t] += jnp.dot(hidden, down[:, span], preferred_element_type=jnp.float32)
        in_acc[t] += lax.dot_general(grad_pre, up[span, :], NT, preferred_element_type=jnp.float32)

    @pl.when(step == pl.num_programs(0) - 1)
    def _():
        part[:, 0] = out_acc[...].astype(jnp.bfloat16)
        part[:, 1] = in_acc[...].astype(jnp.bfloat16)


def layer(x, up, down):
    owners, _, count_tok, feats = x.shape
    width, hidden = up.shape
    block = min(256, hidden)
    whole = pl.BlockSpec(x.shape, lambda h: (0, 0, 0, 0), pipeline_mode=pl.Buffered(1))
    return pl.pallas_call(
        layer_kernel,
        grid=(hidden // block,),
        out_shape=(
            jax.ShapeDtypeStruct((2, count_tok, hidden), jnp.bfloat16),
            jax.ShapeDtypeStruct(x.shape, jnp.bfloat16),
        ),
        in_specs=[
            whole,
            pl.BlockSpec((width, block), lambda h: (0, h)),
            pl.BlockSpec((block, width), lambda h: (h, 0)),
        ],
        out_specs=(
            pl.BlockSpec((2, count_tok, block), lambda h: (0, 0, h)),
            pl.BlockSpec(x.shape, lambda h: (0, 0, 0, 0)),
        ),
        scratch_shapes=[pltpu.VMEM((owners, count_tok, feats), jnp.float32)] * 2,
        compiler_params=pltpu.CompilerParams(vmem_limit_bytes=VMEM_LIMIT),
        cost_estimate=pl.CostEstimate(
            flops=8 * count_tok * width * hidden, bytes_accessed=4 * width * hidden, transcendentals=0
        ),
        name="layer",
    )(x, up, down)


def grads_kernel(scale, rows, cols, info, x, hg, grad_up, grad_down):
    group, side = grad_up.shape[0], grad_up.shape[1]
    per = x.shape[4] // side
    base = info[1] + pl.program_id(0) * group

    for j in range(group):
        s = base + j
        live = s < info[0]

        @pl.when(live)
        def _():
            r = pl.multiple_of(rows[s] * side, side)
            c = cols[s]
            owner = c // per
            f = pl.multiple_of((c - owner * per) * side, side)
            tokens = x.shape[0] * x.shape[3]
            xs = x[:, owner, 0, :, pl.ds(f, side)].reshape(tokens, side)
            dys = x[:, owner, 1, :, pl.ds(f, side)].reshape(tokens, side)
            h = hg[:, 0, :, pl.ds(r, side)].reshape(tokens, side)
            g = hg[:, 1, :, pl.ds(r, side)].reshape(tokens, side)
            grad_up[j] = lax.dot_general(xs, g, TN, preferred_element_type=jnp.float32) * scale
            grad_down[j] = lax.dot_general(h, dys, TN, preferred_element_type=jnp.float32) * scale

        @pl.when(jnp.logical_not(live))
        def _():
            grad_up[j] = jnp.zeros((side, side), jnp.float32)
            grad_down[j] = jnp.zeros((side, side), jnp.float32)


def grads(rows, cols, info, x, hg, slots, side, scale):
    smem = pl.BlockSpec(memory_space=pltpu.SMEM)
    group = min(8, slots)
    out = pl.BlockSpec((group, side, side), lambda i: (i, 0, 0))
    shape = jax.ShapeDtypeStruct((slots, side, side), jnp.float32)
    return pl.pallas_call(
        functools.partial(grads_kernel, scale),
        grid=(slots // group,),
        out_shape=(shape, shape),
        in_specs=[
            smem,
            smem,
            smem,
            pl.BlockSpec(x.shape, lambda i: (0,) * 5, pipeline_mode=pl.Buffered(1)),
            pl.BlockSpec(hg.shape, lambda i: (0,) * 4, pipeline_mode=pl.Buffered(1)),
        ],
        out_specs=(out, out),
        compiler_params=pltpu.CompilerParams(vmem_limit_bytes=VMEM_LIMIT),
        cost_estimate=pl.CostEstimate(
            flops=4 * slots * side * side * x.shape[0] * x.shape[3],
            bytes_accessed=8 * slots * side * side + 2 * x.size + 2 * hg.size,
            transcendentals=0,
        ),
        name="grads",
    )(rows, cols, info, x, hg)


def body(tokens, grad_out, up_tiles, down_tiles, tile_rows, tile_cols, tile_count):
    slots, side = up_tiles.shape[1:3]
    n_tile, n_dp = lax.axis_size("tile"), lax.axis_size("dp")
    hidden = HIDDEN_SIZE // n_tile
    width = tokens.shape[1] * n_tile
    mine = jnp.stack([tokens, grad_out])
    x = lax.all_gather(mine, "tile")
    up, down = densify(tile_rows[0], tile_cols[0], tile_count, up_tiles[0], down_tiles[0], width, hidden)
    x_all = lax.all_gather(x, "dp")
    hg, part = layer(x, up, down)
    hg_all = lax.all_gather(hg, "dp")
    total = lax.psum_scatter(part, "tile", scatter_dimension=0)
    share = slots // n_dp
    info = jnp.concatenate([tile_count, (lax.axis_index("dp") * share).astype(jnp.int32)[None]])
    grad_up, grad_down = grads(tile_rows[0], tile_cols[0], info, x_all, hg_all, share, side, 1.0 / n_dp)
    return (total[0], total[1], grad_up[None], grad_down[None])


def solution(mesh):
    placed = (
        P("dp", "tile"),
        P("dp", "tile"),
        P("tile", None, None, None),
        P("tile", None, None, None),
        P("tile", None),
        P("tile", None),
        P("tile"),
    )
    return jax.shard_map(
        body,
        mesh=mesh,
        in_specs=placed,
        out_specs=(
            P("dp", "tile"),
            P("dp", "tile"),
            P("tile", "dp", None, None),
            P("tile", "dp", None, None),
        ),
        check_vma=False,
    )
```

time: 403 us -> 278 us (0.69)
  the two profiles are of different devices: /device:TPU:0 before, /device:TPU:1 now
where the time goes in v1:
time: 278 us; the launch traced here: 277 us
  waiting for transfers between devices  190 us (68%)
  Pallas kernels  68.6 us (25%)
  between operations  14.4 us (5%)
    all_gather x1, waiting for transfers between devices, body(): x_all = lax.all_gather(x, 'dp')  89.2 us
    all_gather x1, waiting for transfers between devices, body(): hg_all = lax.all_gather(hg, 'dp')  54.5 us
    reduce_scatter x1, waiting for transfers between devices, body(): total = lax.psum_scatter(part, 'tile', scatter_dimension=0)  30.5 us
    pallas_call x1, Pallas kernels, grads(): pl.pallas_call(functools.partial(grads_kernel, scale), grid=(slots // gro...  26.1 us
    pallas_call x1, Pallas kernels, layer(): pl.pallas_call(layer_kernel, grid=(hidden // block,), out_shape=(jax.Shap...  24.9 us
    pallas_call x1, Pallas kernels, densify(): pl.pallas_call(dense_kernel, out_shape=(jax.ShapeDtypeStruct((width, hidd...  17.6 us
    all_gather x1, waiting for transfers between devices, body(): x = lax.all_gather(mine, 'tile')  14.6 us
  transfers between devices with their start and end apart: 4, of which 4 were waited for; matrix products, arithmetic and copies ran while one was open for 1% of the time, Pallas kernels for 6%

profile of v1, /device:TPU:1, one launch (start us, length us, event | category | flops | bytes accessed | tf_op | source)
XLA Modules:
  0.0 277.2 jit_solution(14382509806934444891)
XLA Ops:
  7.2 0.0 all-gather.7.cloned.1.call-start
  7.2 1.7 pad_maximum_fusion
  8.9 0.0 all-gather.7.cloned.1.call-update
  8.9 0.0 reduce-scatter.2.cloned.1.call-start
  9.6 17.6 %densify.1 = (bf16[4096,2048]{1,0:T(8,128)(2,1)}, bf16[2048,4096]{1,0:T(8,128)(2,1)}) custom-call(s32[256]{0:T(256)} %bitcast.24, s32[256]{0:T(256)} %bitcast.26, s32[1]{0:T(128)S(6)} %copy.11.count, bf16[256,128,128]{2,1,0:T(8,128)(2,1)} %bitcast.19, bf16[256,128,128]{2,1,0:T(8,128)(2,1)} %bitcast.20), custom_call_target="tpu_custom_call" | custom-call | bytes 50331648 | tf_op jit(solution)/shard_map/densify/pallas_call | solution.py:74
  27.2 14.6 %all-gather.7.cloned.1.call-done = bf16[16,128,512]{2,1,0:T(8,128)(2,1)} async-done(((bf16[2,128,512]{2,1,0:T(8,128)(2,1)}), bf16[16,128,512]{2,1,0:T(8,128)(2,1)}) %all-gather.7.cloned.1.call-update) | async-done | bytes 2097168 | tf_op jit(solution)/shard_map/all_gather | solution.py:221
  41.8 24.9 %layer.1 = (bf16[2,128,2048]{2,1,0:T(8,128)(2,1)}, bf16[8,2,128,512]{3,2,1,0:T(8,128)(2,1)}) custom-call(bf16[8,2,128,512]{3,2,1,0:T(8,128)(2,1)} %bitcast.16, bf16[4096,2048]{1,0:T(8,128)(2,1)} %get-tuple-element.10.up, bf16[2048,4096]{1,0:T(8,128)(2,1)} %get-tuple-element.11.down), custom_call_target="tpu_custom_call" | custom-call | flops 8589934592 | bytes 33554432 | tf_op jit(solution)/shard_map/layer/pallas_call | solution.py:134
  66.7 0.0 reduce-scatter.2.cloned.1.call-update
  66.8 0.0 all-gather.11.cloned.1.call-start
  66.8 0.7 all-gather.11.cloned.1.call-update
  67.5 0.0 all-gather.9.cloned.1.call-start
  67.5 0.5 all-gather.9.cloned.1.call-update
  68.1 0.6 pad_add_fusion.info
  68.6 30.5 %reduce-scatter.2.cloned.1.call-done = bf16[1,2,128,512]{3,2,1,0:T(8,128)(2,1)} async-done(((bf16[8,2,128,512]{3,2,1,0:T(8,128)(2,1)}), bf16[1,2,128,512]{3,2,1,0:T(8,128)(2,1)}) %reduce-scatter.2.cloned.1.call-update) | async-done | bytes 262160 | tf_op jit(solution)/shard_map/reduce_scatter | solution.py:226
  99.2 1.7 slice_bitcast_fusion
  100.8 54.5 %all-gather.11.cloned.1.call-done = bf16[8,128,2048]{2,1,0:T(8,128)(2,1)} async-done(((bf16[2,128,2048]{2,1,0:T(8,128)(2,1)}), bf16[8,128,2048]{2,1,0:T(8,128)(2,1)}) %all-gather.11.cloned.1.call-update) | async-done | bytes 4194320 | tf_op jit(solution)/shard_map/all_gather | solution.py:225
  155.3 89.2 %all-gather.9.cloned.1.call-done = bf16[32,2,128,512]{3,2,1,0:T(8,128)(2,1)} async-done(((bf16[8,2,128,512]{3,2,1,0:T(8,128)(2,1)}), bf16[32,2,128,512]{3,2,1,0:T(8,128)(2,1)}) %all-gather.9.cloned.1.call-update) | async-done | bytes 8388624 | tf_op jit(solution)/shard_map/all_gather | solution.py:223
  244.5 26.1 %grads.1 = (f32[64,128,128]{2,1,0:T(8,128)}, f32[64,128,128]{2,1,0:T(8,128)}) custom-call(s32[256]{0:T(256)} %bitcast.25, s32[256]{0:T(256)} %bitcast.27, s32[2]{0:T(128)} %pad_add_fusion.info, bf16[4,8,2,128,512]{4,3,2,1,0:T(8,128)(2,1)} %bitcast.18, bf16[4,2,128,2048]{3,2,1,0:T(8,128)(2,1)} %bitcast.21), custom_call_target="tpu_custom_call" | custom-call | flops 2147483648 | bytes 20971520 | tf_op jit(solution)/shard_map/grads/pallas_call | solution.py:193
Async XLA Ops:
  7.2 34.6 %all-gather.7.cloned.1.call-start = ((), (), s32[]{:S(2)}) async-start(), calls=%async_computation.2 | async-start | bytes 2359296 | tf_op jit(solution)/shard_map/all_gather | solution.py:221
  8.9 90.2 %reduce-scatter.2.cloned.1.call-start = ((), (), s32[]{:S(2)}) async-start(), calls=%async_computation.1 | async-start | bytes 2359296 | tf_op jit(solution)/shard_map/reduce_scatter | solution.py:226
  66.8 88.6 %all-gather.11.cloned.1.call-start = ((), (), s32[]{:S(2)}) async-start(), calls=%async_computation.4 | async-start | bytes 5242880 | tf_op jit(solution)/shard_map/all_gather | solution.py:225
  67.5 177.0 %all-gather.9.cloned.1.call-start = ((), (), s32[]{:S(2)}) async-start(), calls=%async_computation.3 | async-start | bytes 10485760 | tf_op jit(solution)/shard_map/all_gather | solution.py:223
Sparse Core Ops, SparseCore 0:
  10.1 31.6 all-gather.6
  66.9 32.2 reduce-scatter.1
  101.6 53.6 all-gather.10
  157.0 87.4 all-gather.8

commit v2 on v1

--- a/solution.py
+++ b/solution.py
@@ -95,65 +95,193 @@
 TN = (((0,), (0,)), ((), ()))
 
 
-def layer_kernel(x, up, down, hg, part, out_acc, in_acc):
-    step = pl.program_id(0)
-    owners, _, _, feats = x.shape
-
-    @pl.when(step == 0)
-    def _():
-        out_acc[...] = jnp.zeros_like(out_acc)
-        in_acc[...] = jnp.zeros_like(in_acc)
-
-    pre = jnp.zeros(hg.shape[1:], jnp.float32)
-    grad_hidden = jnp.zeros(hg.shape[1:], jnp.float32)
-    for t in range(owners):
-        span = slice(t * feats, (t + 1) * feats)
-        pre += jnp.dot(x[t, 0], up[span, :], preferred_element_type=jnp.float32)
-        grad_hidden += lax.dot_general(x[t, 1], down[:, span], NT, preferred_element_type=jnp.float32)
-    value, slope = gelu_pair(pre)
-    hidden = value.astype(jnp.bfloat16)
-    grad_pre = (grad_hidden * slope).astype(jnp.bfloat16)
-    hg[0] = hidden
-    hg[1] = grad_pre
-    for t in range(owners):
-        span = slice(t * feats, (t + 1) * feats)
-        out_acc[t] += jnp.dot(hidden, down[:, span], preferred_element_type=jnp.float32)
-        in_acc[t] += lax.dot_general(grad_pre, up[span, :], NT, preferred_element_type=jnp.float32)
-
-    @pl.when(step == pl.num_programs(0) - 1)
-    def _():
-        part[:, 0] = out_acc[...].astype(jnp.bfloat16)
-        part[:, 1] = in_acc[...].astype(jnp.bfloat16)
-
-
-def layer(x, up, down):
-    owners, _, count_tok, feats = x.shape
+def layer_kernel(n_dp, n_tile, mine, up, down, x_all, hg_all, part,
+                 xz, up_v, down_v, pre, hg, outbox, inbox,
+                 up_sem, down_sem, own_sem, z_send, z_recv, f_send, f_recv, d_send, d_recv, e_send, e_recv,
+                 h_send, h_recv, r_send, r_recv):
+    n_z = n_tile // 2
+    dp = lax.axis_index("dp")
+    me = lax.axis_index("tile")
+    z, core = me // 2, me % 2
+    sib = 2 * z + (1 - core)
+    feats = xz.shape[3]
+    hidden = pre.shape[2]
+    block = min(256, hidden)
+
+    def to(src, dst, ssem, rsem, d, t):
+        return pltpu.make_async_remote_copy(
+            src_ref=src, dst_ref=dst, send_sem=ssem, recv_sem=rsem,
+            device_id={"dp": d, "tile": t}, device_id_type=pl.DeviceIdType.MESH)
+
+    def owner(j):
+        return 2 * ((z + n_z - j) % n_z) + core
+
+    def other(j):
+        return 2 * ((z + n_z - j) % n_z) + 1 - core
+
+    def up_copy(t):
+        return pltpu.make_async_copy(up.at[t], up_v.at[t], up_sem.at[t])
+
+    def down_copy(t):
+        at = pl.ds(pl.multiple_of(t * feats, 128), feats)
+        return pltpu.make_async_copy(down.at[:, at], down_v.at[t], down_sem.at[t])
+
+    def z_copy(j):
+        return to(xz.at[me], xz.at[me], z_send.at[j], z_recv.at[j], dp, 2 * ((z + j) % n_z) + core)
+
+    def f_copy(j):
+        return to(xz.at[owner(j)], xz.at[owner(j)], f_send.at[j], f_recv.at[j], dp, sib)
+
+    def d_copy(k, j):
+        return to(xz.at[owner(j)], x_all.at[dp, owner(j)], d_send.at[k, j], d_recv.at[k, j], (dp + k) % n_dp, me)
+
+    def e_copy(k, j):
+        slot = x_all.at[(dp + n_dp - k) % n_dp, owner(j)]
+        return to(slot, slot, e_send.at[k, j], e_recv.at[k, j], dp, sib)
+
+    def h_copy(k):
+        return to(hg, hg_all.at[dp], h_send.at[k], h_recv.at[k], (dp + k) % n_dp, me)
+
+    def r_copy(i):
+        return to(outbox.at[i], inbox.at[i], r_send.at[i], r_recv.at[i], dp, (me + i) % n_tile)
+
+    barrier = pltpu.get_barrier_semaphore()
+    for i in range(1, n_tile):
+        pl.semaphore_signal(barrier, inc=1, device_id={"dp": dp, "tile": (me + i) % n_tile},
+                            device_id_type=pl.DeviceIdType.MESH)
+    for k in range(1, n_dp):
+        pl.semaphore_signal(barrier, inc=1, device_id={"dp": (dp + k) % n_dp, "tile": me},
+                            device_id_type=pl.DeviceIdType.MESH)
+    own = pltpu.make_async_copy(mine, xz.at[me], own_sem.at[0])
+    own.start()
+    for j in range(n_z):
+        for t in (owner(j), other(j)):
+            up_copy(t).start()
+            down_copy(t).start()
+    pre[...] = jnp.zeros_like(pre)
+    pl.semaphore_wait(barrier, n_tile + n_dp - 2)
+    own.wait()
+    for j in range(1, n_z):
+        z_copy(j).start()
+    f_copy(0).start()
+    for k in range(1, n_dp):
+        d_copy(k, 0).start()
+
+    def gather_in(t):
+        up_copy(t).wait()
+        down_copy(t).wait()
+
+        @pl.loop(0, hidden // block)
+        def _(b):
+            at = pl.ds(pl.multiple_of(b * block, block), block)
+            pre[0, :, at] += jnp.dot(xz[t, 0], up_v[t, :, at], preferred_element_type=jnp.float32)
+            pre[1, :, at] += lax.dot_general(xz[t, 1], down_v[t, at, :], NT, preferred_element_type=jnp.float32)
+
+    for j in range(n_z):
+        if j:
+            z_copy(j).wait_recv()
+            f_copy(j).start()
+            for k in range(1, n_dp):
+                d_copy(k, j).start()
+        gather_in(owner(j))
+        f_copy(j).wait_recv()
+        gather_in(other(j))
+
+    @pl.loop(0, hidden // block)
+    def _(b):
+        at = pl.ds(pl.multiple_of(b * block, block), block)
+        value, slope = gelu_pair(pre[0, :, at])
+        hg[0, :, at] = value.astype(jnp.bfloat16)
+        hg[1, :, at] = (pre[1, :, at] * slope).astype(jnp.bfloat16)
+
+    for k in range(1, n_dp):
+        h_copy(k).start()
+    keep_hg = pltpu.make_async_copy(hg, hg_all.at[dp], own_sem.at[1])
+    keep_hg.start()
+    keep_x = pltpu.make_async_copy(xz, x_all.at[dp], own_sem.at[2])
+    keep_x.start()
+
+    def terms(i):
+        t = (me + i) % n_tile
+        outbox[i, 0] = jnp.dot(hg[0], down_v[t], preferred_element_type=jnp.float32).astype(jnp.bfloat16)
+        outbox[i, 1] = lax.dot_general(hg[1], up_v[t], NT, preferred_element_type=jnp.float32).astype(jnp.bfloat16)
+
+    @pl.loop(1, n_tile)
+    def _(i):
+        terms(i)
+        r_copy(i).start()
+
+    terms(0)
+    for j in range(n_z):
+        for k in range(1, n_dp):
+            d_copy(k, j).wait_recv()
+            e_copy(k, j).start()
+    total = outbox[0].astype(jnp.float32)
+    for i in range(1, n_tile):
+        r_copy(i).wait_recv()
+        total = total + inbox[i].astype(jnp.float32)
+    part[...] = total.astype(jnp.bfloat16)
+    keep_hg.wait()
+    keep_x.wait()
+    for j in range(n_z):
+        if j:
+            z_copy(j).wait_send()
+        f_copy(j).wait_send()
+        for k in range(1, n_dp):
+            d_copy(k, j).wait_send()
+            e_copy(k, j).wait()
+    for k in range(1, n_dp):
+        h_copy(k).wait()
+    for i in range(1, n_tile):
+        r_copy(i).wait_send()
+
+
+def layer(mine, up, down, n_dp, n_tile):
+    _, count_tok, feats = mine.shape
     width, hidden = up.shape
-    block = min(256, hidden)
-    whole = pl.BlockSpec(x.shape, lambda h: (0, 0, 0, 0), pipeline_mode=pl.Buffered(1))
+    n_z = n_tile // 2
+    hbm = pl.BlockSpec(memory_space=pl.ANY)
+    kind = jnp.bfloat16
+    dma = pltpu.SemaphoreType.DMA
+    box = pltpu.VMEM((n_tile, 2, count_tok, feats), kind)
     return pl.pallas_call(
-        layer_kernel,
-        grid=(hidden // block,),
+        functools.partial(layer_kernel, n_dp, n_tile),
         out_shape=(
-            jax.ShapeDtypeStruct((2, count_tok, hidden), jnp.bfloat16),
-            jax.ShapeDtypeStruct(x.shape, jnp.bfloat16),
-        ),
-        in_specs=[
-            whole,
-            pl.BlockSpec((width, block), lambda h: (0, h)),
-            pl.BlockSpec((block, width), lambda h: (h, 0)),
+            jax.ShapeDtypeStruct((n_dp, n_tile, 2, count_tok, feats), kind),
+            jax.ShapeDtypeStruct((n_dp, 2, count_tok, hidden), kind),
+            jax.ShapeDtypeStruct(mine.shape, kind),
+        ),
+        in_specs=[hbm, hbm, hbm],
+        out_specs=(hbm, hbm, pl.BlockSpec(memory_space=pltpu.VMEM)),
+        scratch_shapes=[
+            box,
+            pltpu.VMEM((n_tile, feats, hidden), kind),
+            pltpu.VMEM((n_tile, hidden, feats), kind),
+            pltpu.VMEM((2, count_tok, hidden), jnp.float32),
+            pltpu.VMEM((2, count_tok, hidden), kind),
+            box,
+            box,
+            dma((n_tile,)),
+            dma((n_tile,)),
+            dma((3,)),
+            dma((n_z,)),
+            dma((n_z,)),
+            dma((n_z,)),
+            dma((n_z,)),
+            dma((n_dp, n_z)),
+            dma((n_dp, n_z)),
+            dma((n_dp, n_z)),
+            dma((n_dp, n_z)),
+            dma((n_dp,)),
+            dma((n_dp,)),
+            dma((n_tile,)),
+            dma((n_tile,)),
         ],
-        out_specs=(
-            pl.BlockSpec((2, count_tok, block), lambda h: (0, 0, h)),
-            pl.BlockSpec(x.shape, lambda h: (0, 0, 0, 0)),
-        ),
-        scratch_shapes=[pltpu.VMEM((owners, count_tok, feats), jnp.float32)] * 2,
-        compiler_params=pltpu.CompilerParams(vmem_limit_bytes=VMEM_LIMIT),
-        cost_estimate=pl.CostEstimate(
-            flops=8 * count_tok * width * hidden, bytes_accessed=4 * width * hidden, transcendentals=0
+        compiler_params=pltpu.CompilerParams(
+            vmem_limit_bytes=VMEM_LIMIT, collective_id=0, has_side_effects=True
         ),
         name="layer",
-    )(x, up, down)
+    )(mine, up.reshape(n_tile, feats, hidden), down)
 
 
 def grads_kernel(scale, rows, cols, info, x, hg, grad_up, grad_down):
@@ -218,12 +346,8 @@
     hidden = HIDDEN_SIZE // n_tile
     width = tokens.shape[1] * n_tile
     mine = jnp.stack([tokens, grad_out])
-    x = lax.all_gather(mine, "tile")
     up, down = densify(tile_rows[0], tile_cols[0], tile_count, up_tiles[0], down_tiles[0], width, hidden)
-    x_all = lax.all_gather(x, "dp")
-    hg, part = layer(x, up, down)
-    hg_all = lax.all_gather(hg, "dp")
-    total = lax.psum_scatter(part, "tile", scatter_dimension=0)
+    x_all, hg_all, total = layer(mine, up, down, n_dp, n_tile)
     share = slots // n_dp
     info = jnp.concatenate([tile_count, (lax.axis_index("dp") * share).astype(jnp.int32)[None]])
     grad_up, grad_down = grads(tile_rows[0], tile_cols[0], info, x_all, hg_all, share, side, 1.0 / n_dp)

time: 278 us -> 155 us (0.56)
  the two profiles are of different devices: /device:TPU:1 before, /device:TPU:16 now
where the time goes in v2:
time: 155 us; the launch traced here: 153 us
  Pallas kernels  148 us (95%)
  other arithmetic  2.3 us (1%)
  local copies, waits for them, and re-layouts  1.68 us (1%)
    pallas_call x1, Pallas kernels, layer(): pl.pallas_call(functools.partial(layer_kernel, n_dp, n_tile), out_shape=(...  106 us
    pallas_call x1, Pallas kernels, grads(): pl.pallas_call(functools.partial(grads_kernel, scale), grid=(slots // gro...  25.8 us
    pallas_call x1, Pallas kernels, densify(): pl.pallas_call(dense_kernel, out_shape=(jax.ShapeDtypeStruct((width, hidd...  15.9 us

profile of v2, /device:TPU:16, one launch (start us, length us, event | category | flops | bytes accessed | tf_op | source)
XLA Modules:
  0.0 153.1 jit_solution(13298275127985990468)
XLA Ops:
  1.3 0.6 pad_add_fusion.info
  1.9 1.7 %pad_maximum_fusion.mine = bf16[2,128,512]{2,1,0:T(8,128)(2,1)} fusion(bf16[1,128,512]{2,1,0:T(8,128)(2,1)} %bitcast.17, bf16[1,128,512]{2,1,0:T(8,128)(2,1)} %bitcast.18), kind=kLoop, calls=%fused_computation | loop fusion | flops 131072 | bytes 524288 | tf_op jit(solution)/shard_map/stack | solution.py:348
  3.6 15.9 %densify.1 = (bf16[4096,2048]{1,0:T(8,128)(2,1)}, bf16[2048,4096]{1,0:T(8,128)(2,1)}) custom-call(s32[256]{0:T(256)} %bitcast.19, s32[256]{0:T(256)} %bitcast.21, s32[1]{0:T(128)S(6)} %copy.11.count, bf16[256,128,128]{2,1,0:T(8,128)(2,1)} %bitcast.15, bf16[256,128,128]{2,1,0:T(8,128)(2,1)} %bitcast.16), custom_call_target="tpu_custom_call" | custom-call | bytes 50331648 | tf_op jit(solution)/shard_map/densify/pallas_call | solution.py:74
  19.5 106.1 %layer.1 = (bf16[4,8,2,128,512]{4,3,2,1,0:T(8,128)(2,1)}, bf16[4,2,128,2048]{3,2,1,0:T(8,128)(2,1)}, bf16[2,128,512]{2,1,0:T(8,128)(2,1)}) custom-call(bf16[2,128,512]{2,1,0:T(8,128)(2,1)} %pad_maximum_fusion.mine, bf16[8,512,2048]{2,1,0:T(8,128)(2,1)} %bitcast.14, bf16[2048,4096]{1,0:T(8,128)(2,1)} %get-tuple-element.12.down), custom_call_target="tpu_custom_call" | custom-call | tf_op jit(solution)/shard_map/layer/pallas_call | solution.py:247
  125.6 1.7 %slice_bitcast_fusion = (bf16[128,512]{1,0:T(8,128)(2,1)}, bf16[128,512]{1,0:T(8,128)(2,1)}) fusion(bf16[2,128,512]{2,1,0:T(8,128)(2,1)} %get-tuple-element.13), kind=kLoop, calls=%fused_computation.1 | loop fusion | bytes 524288 | tf_op jit(solution)/shard_map/squeeze | solution.py:354
  127.3 25.8 %grads.1 = (f32[64,128,128]{2,1,0:T(8,128)}, f32[64,128,128]{2,1,0:T(8,128)}) custom-call(s32[256]{0:T(256)} %bitcast.20, s32[256]{0:T(256)} %bitcast.22, s32[2]{0:T(128)} %pad_add_fusion.info, bf16[4,8,2,128,512]{4,3,2,1,0:T(8,128)(2,1)} %get-tuple-element.14.x, bf16[4,2,128,2048]{3,2,1,0:T(8,128)(2,1)} %get-tuple-element.15.hg), custom_call_target="tpu_custom_call" | custom-call | flops 2147483648 | bytes 20971520 | tf_op jit(solution)/shard_map/grads/pallas_call | solution.py:321

commit v3 on v2

v3 whole, which is shorter than its diff:
```python
import functools

import jax
import jax.numpy as jnp
from jax import lax
from jax.experimental import pallas as pl
from jax.experimental.pallas import tpu as pltpu
from jax.sharding import PartitionSpec as P

HIDDEN_SIZE = 16384
VMEM_LIMIT = 64 * 1024 * 1024 - 65536


def gelu_pair(pre):
    curve = lax.erf(pre * 0.7071067811865476)
    value = 0.5 * pre * (1.0 + curve)
    slope = 0.5 * (1.0 + curve) + pre * jnp.exp(-0.5 * pre * pre) * 0.3989422804014327
    return (value, slope)


NT = (((1,), (1,)), ((), ()))
TN = (((0,), (0,)), ((), ()))


def layer_kernel(n_dp, n_tile, slot_of, tokens, grad_out, up, down, x_all, hg_all, mixed, grad_in,
                 xz, up_t, down_t, up_v, down_v, pre, hg, outbox, inbox,
                 own_sem, z_send, z_recv, f_send, f_recv, d_send, d_recv, l_send, l_recv, e_send, e_recv,
                 h_send, h_recv, m_send, m_recv, r_send, r_recv):
    n_z = n_tile // 2
    dp = lax.axis_index("dp")
    me = lax.axis_index("tile")
    z, core = me // 2, me % 2
    sib = 2 * z + (1 - core)
    feats = xz.shape[3]
    hidden = pre.shape[2]
    slots, side = up.shape[0], up.shape[1]
    block = min(256, hidden)
    pieces = hg.shape[0]
    piece = hg.shape[3]
    square = n_dp == 4
    if square:
        x_next = 2 * (dp // 2) + 1 - dp % 2
        y_next = 2 * (1 - dp // 2) + dp % 2
        across = n_dp - 1 - dp
        targets = sources = [x_next, y_next]
        arrivals = [x_next, y_next, across]
    else:
        targets = [(dp + k) % n_dp for k in range(1, n_dp)]
        sources = arrivals = [(dp + n_dp - k) % n_dp for k in range(1, n_dp)]
    direct = range(len(targets))

    def to(src, dst, ssem, rsem, d, t):
        return pltpu.make_async_remote_copy(
            src_ref=src, dst_ref=dst, send_sem=ssem, recv_sem=rsem,
            device_id={"dp": d, "tile": t}, device_id_type=pl.DeviceIdType.MESH)

    def owner(j):
        return 2 * ((z + n_z - j) % n_z) + core

    def other(j):
        return 2 * ((z + n_z - j) % n_z) + 1 - core

    def z_copy(j):
        return to(xz.at[me], xz.at[me], z_send.at[j], z_recv.at[j], dp, 2 * ((z + j) % n_z) + core)

    def f_copy(j):
        return to(xz.at[owner(j)], xz.at[owner(j)], f_send.at[j], f_recv.at[j], dp, sib)

    def d_copy(k, j):
        return to(xz.at[owner(j)], x_all.at[dp, owner(j)], d_send.at[k, j], d_recv.at[k, j], targets[k], me)

    def l_copy(k, j):
        slot = x_all.at[sources[k], owner(j), k]
        return to(slot, slot, l_send.at[k, j], l_recv.at[k, j], targets[1 - k], me)

    def e_copy(k, j):
        slot = x_all.at[arrivals[k], owner(j)]
        return to(slot, slot, e_send.at[k, j], e_recv.at[k, j], dp, sib)

    def h_copy(k, p):
        return to(hg.at[p], hg_all.at[dp, p], h_send.at[k, p], h_recv.at[k, p], targets[k], me)

    def m_copy(k, p):
        slot = hg_all.at[sources[k], p, k]
        return to(slot, slot, m_send.at[k, p], m_recv.at[k, p], targets[1 - k], me)

    def r_copy(i):
        return to(outbox.at[i], inbox.at[i], r_send.at[i], r_recv.at[i], dp, (me + i) % n_tile)

    def landed(j):
        for k in direct:
            d_copy(k, j).wait_recv()
            if square:
                l_copy(k, j).start()
            e_copy(k, j).start()

    barrier = pltpu.get_barrier_semaphore()
    for i in range(1, n_tile):
        pl.semaphore_signal(barrier, inc=1, device_id={"dp": dp, "tile": (me + i) % n_tile},
                            device_id_type=pl.DeviceIdType.MESH)
    for k in direct:
        pl.semaphore_signal(barrier, inc=1, device_id={"dp": targets[k], "tile": me},
                            device_id_type=pl.DeviceIdType.MESH)
    own = [pltpu.make_async_copy(tokens, xz.at[me, 0], own_sem.at[0]),
           pltpu.make_async_copy(grad_out, xz.at[me, 1], own_sem.at[1])]
    load = [pltpu.make_async_copy(up, up_t.at[pl.ds(0, slots)], own_sem.at[2]),
            pltpu.make_async_copy(down, down_t.at[pl.ds(0, slots)], own_sem.at[3])]
    for copy in own + load:
        copy.start()
    up_t[slots] = jnp.zeros((side, side), up_t.dtype)
    down_t[slots] = jnp.zeros((side, side), down_t.dtype)
    pre[...] = jnp.zeros_like(pre)
    pl.semaphore_wait(barrier, n_tile - 1 + len(targets))
    for copy in own:
        copy.wait()
    for j in range(1, n_z):
        z_copy(j).start()
    f_copy(0).start()
    for k in direct:
        d_copy(k, 0).start()
    for copy in load:
        copy.wait()

    def gather_in(t):
        wide = feats // side
        high = hidden // side

        @pl.loop(0, high)
        def _(r):
            at = pl.ds(pl.multiple_of(r * side, side), side)
            for c in range(wide):
                slot = slot_of[(t * wide + c) * high + r]
                up_v[t, c * side:(c + 1) * side, at] = up_t[slot]
                down_v[t, at, c * side:(c + 1) * side] = down_t[slot]

        @pl.loop(0, hidden // block)
        def _(b):
            at = pl.ds(pl.multiple_of(b * block, block), block)
            pre[0, :, at] += jnp.dot(xz[t, 0], up_v[t, :, at], preferred_element_type=jnp.float32)
            pre[1, :, at] += lax.dot_general(xz[t, 1], down_v[t, at, :], NT, preferred_element_type=jnp.float32)

    for j in range(n_z):
        if j:
            z_copy(j).wait_recv()
            f_copy(j).start()
            for k in direct:
                d_copy(k, j).start()
        gather_in(owner(j))
        f_copy(j).wait_recv()
        gather_in(other(j))
        if j:
            landed(j - 1)

    for p in range(pieces):
        value, slope = gelu_pair(pre[0, :, p * piece:(p + 1) * piece])
        hg[p, 0] = value.astype(jnp.bfloat16)
        hg[p, 1] = (pre[1, :, p * piece:(p + 1) * piece] * slope).astype(jnp.bfloat16)
        for k in direct:
            h_copy(k, p).start()
    keep = [pltpu.make_async_copy(hg, hg_all.at[dp], own_sem.at[0]),
            pltpu.make_async_copy(xz, x_all.at[dp], own_sem.at[1])]
    for copy in keep:
        copy.start()

    def terms(i):
        t = (me + i) % n_tile
        out = jnp.zeros((pre.shape[1], feats), jnp.float32)
        back = jnp.zeros((pre.shape[1], feats), jnp.float32)
        for p in range(pieces):
            span = slice(p * piece, (p + 1) * piece)
            out += jnp.dot(hg[p, 0], down_v[t, span, :], preferred_element_type=jnp.float32)
            back += lax.dot_general(hg[p, 1], up_v[t, :, span], NT, preferred_element_type=jnp.float32)
        outbox[i, 0] = out.astype(jnp.bfloat16)
        outbox[i, 1] = back.astype(jnp.bfloat16)

    @pl.loop(1, n_tile)
    def _(i):
        terms(i)
        r_copy(i).start()

    landed(n_z - 1)
    terms(0)
    for p in range(pieces):
        if square:
            for k in direct:
                h_copy(k, p).wait_recv()
                m_copy(k, p).start()
    if square:
        for j in range(n_z):
            for k in direct:
                l_copy(k, j).wait_recv()
            e_copy(2, j).start()
    mix = outbox[0, 0].astype(jnp.float32)
    back = outbox[0, 1].astype(jnp.float32)
    for i in range(1, n_tile):
        r_copy(i).wait_recv()
        mix = mix + inbox[i, 0].astype(jnp.float32)
        back = back + inbox[i, 1].astype(jnp.float32)
    mixed[...] = mix.astype(jnp.bfloat16)
    grad_in[...] = back.astype(jnp.bfloat16)
    for copy in keep:
        copy.wait()
    for j in range(n_z):
        if j:
            z_copy(j).wait_send()
        f_copy(j).wait_send()
        for k in direct:
            d_copy(k, j).wait_send()
            if square:
                l_copy(k, j).wait_send()
        for k in range(n_dp - 1):
            e_copy(k, j).wait()
    for p in range(pieces):
        for k in direct:
            h_copy(k, p).wait_send()
            if square:
                m_copy(k, p).wait()
            else:
                h_copy(k, p).wait_recv()
    for i in range(1, n_tile):
        r_copy(i).wait_send()


def layer(slot_of, tokens, grad_out, up, down, n_dp, n_tile):
    count_tok, feats = tokens.shape
    slots, side = up.shape[:2]
    hidden = HIDDEN_SIZE // n_tile
    n_z = n_tile // 2
    pieces = min(4, hidden // side)
    hbm = pl.BlockSpec(memory_space=pl.ANY)
    vmem = pl.BlockSpec(memory_space=pltpu.VMEM)
    kind = jnp.bfloat16
    dma = pltpu.SemaphoreType.DMA
    box = pltpu.VMEM((n_tile, 2, count_tok, feats), kind)
    packed = (pieces, 2, count_tok, hidden // pieces)
    pairs = [dma((n_dp, n_z)), dma((n_dp, n_z))]
    sends = [dma((n_dp, pieces)), dma((n_dp, pieces))]
    return pl.pallas_call(
        functools.partial(layer_kernel, n_dp, n_tile),
        out_shape=(
            jax.ShapeDtypeStruct((n_dp, n_tile, 2, count_tok, feats), kind),
            jax.ShapeDtypeStruct((n_dp,) + packed, kind),
            jax.ShapeDtypeStruct(tokens.shape, kind),
            jax.ShapeDtypeStruct(tokens.shape, kind),
        ),
        in_specs=[pl.BlockSpec(memory_space=pltpu.SMEM), hbm, hbm, hbm, hbm],
        out_specs=(hbm, hbm, vmem, vmem),
        scratch_shapes=[
            box,
            pltpu.VMEM((slots + 1, side, side), kind),
            pltpu.VMEM((slots + 1, side, side), kind),
            pltpu.VMEM((n_tile, feats, hidden), kind),
            pltpu.VMEM((n_tile, hidden, feats), kind),
            pltpu.VMEM((2, count_tok, hidden), jnp.float32),
            pltpu.VMEM(packed, kind),
            box,
            box,
            dma((4,)),
            dma((n_z,)),
            dma((n_z,)),
            dma((n_z,)),
            dma((n_z,)),
        ] + pairs * 3 + sends * 2 + [
            dma((n_tile,)),
            dma((n_tile,)),
        ],
        compiler_params=pltpu.CompilerParams(
            vmem_limit_bytes=VMEM_LIMIT, collective_id=0, has_side_effects=True
        ),
        name="layer",
    )(slot_of, tokens, grad_out, up, down)


def grads_kernel(scale, rows, cols, info, x, hg, grad_up, grad_down):
    group, side = grad_up.shape[0], grad_up.shape[1]
    per = x.shape[4] // side
    wide = hg.shape[4] // side
    base = info[1] + pl.program_id(0) * group

    for j in range(group):
        s = base + j
        live = s < info[0]

        @pl.when(live)
        def _():
            c = cols[s]
            owner = c // per
            f = pl.multiple_of((c - owner * per) * side, side)
            tokens = x.shape[0] * x.shape[3]
            xs = x[:, owner, 0, :, pl.ds(f, side)].reshape(tokens, side)
            dys = x[:, owner, 1, :, pl.ds(f, side)].reshape(tokens, side)
            p = rows[s] // wide
            r = pl.multiple_of((rows[s] - p * wide) * side, side)
            h = hg[:, p, 0, :, pl.ds(r, side)].reshape(tokens, side)
            g = hg[:, p, 1, :, pl.ds(r, side)].reshape(tokens, side)
            grad_up[j] = lax.dot_general(xs, g, TN, preferred_element_type=jnp.float32) * scale
            grad_down[j] = lax.dot_general(h, dys, TN, preferred_element_type=jnp.float32) * scale

        @pl.when(jnp.logical_not(live))
        def _():
            grad_up[j] = jnp.zeros((side, side), jnp.float32)
            grad_down[j] = jnp.zeros((side, side), jnp.float32)


def grads(rows, cols, info, x, hg, slots, side, scale):
    smem = pl.BlockSpec(memory_space=pltpu.SMEM)
    group = min(8, slots)
    out = pl.BlockSpec((group, side, side), lambda i: (i, 0, 0))
    shape = jax.ShapeDtypeStruct((slots, side, side), jnp.float32)
    return pl.pallas_call(
        functools.partial(grads_kernel, scale),
        grid=(slots // group,),
        out_shape=(shape, shape),
        in_specs=[
            smem,
            smem,
            smem,
            pl.BlockSpec(x.shape, lambda i: (0,) * 5, pipeline_mode=pl.Buffered(1)),
            pl.BlockSpec(hg.shape, lambda i: (0,) * 5, pipeline_mode=pl.Buffered(1)),
        ],
        out_specs=(out, out),
        compiler_params=pltpu.CompilerParams(vmem_limit_bytes=VMEM_LIMIT),
        cost_estimate=pl.CostEstimate(
            flops=4 * slots * side * side * x.shape[0] * x.shape[3],
            bytes_accessed=8 * slots * side * side + 2 * x.size + 2 * hg.size,
            transcendentals=0,
        ),
        name="grads",
    )(rows, cols, info, x, hg)


def body(tokens, grad_out, up_tiles, down_tiles, tile_rows, tile_cols, tile_count):
    slots, side = up_tiles.shape[1:3]
    n_tile, n_dp = lax.axis_size("tile"), lax.axis_size("dp")
    high = HIDDEN_SIZE // (n_tile * side)
    cells = high * (tokens.shape[1] * n_tile // side)
    number = jnp.arange(slots, dtype=jnp.int32)
    place = jnp.where(number < tile_count[0], tile_cols[0] * high + tile_rows[0], -1)
    hit = place[None, :] == jnp.arange(cells, dtype=jnp.int32)[:, None]
    slot_of = jnp.min(jnp.where(hit, number[None, :], slots), axis=1)
    x_all, hg_all, mixed, grad_in = layer(
        slot_of, tokens, grad_out, up_tiles[0], down_tiles[0], n_dp, n_tile
    )
    share = slots // n_dp
    info = jnp.concatenate([tile_count, (lax.axis_index("dp") * share).astype(jnp.int32)[None]])
    grad_up, grad_down = grads(tile_rows[0], tile_cols[0], info, x_all, hg_all, share, side, 1.0 / n_dp)
    return (mixed, grad_in, grad_up[None], grad_down[None])


def solution(mesh):
    placed = (
        P("dp", "tile"),
        P("dp", "tile"),
        P("tile", None, None, None),
        P("tile", None, None, None),
        P("tile", None),
        P("tile", None),
        P("tile"),
    )
    return jax.shard_map(
        body,
        mesh=mesh,
        in_specs=placed,
        out_specs=(
            P("dp", "tile"),
            P("dp", "tile"),
            P("tile", "dp", None, None),
            P("tile", "dp", None, None),
        ),
        check_vma=False,
    )
```

time: 155 us -> 118 us (0.76)
  Pallas kernels: 148 us -> 109 us
    pallas_call x1, Pallas kernels: 106 us -> 84.8 us  [layer(): pl.pallas_call(functools.partial(layer_kernel, n_dp, n_tile), out_shape=(...]
    pallas_call x1 -> x0, Pallas kernels: 15.9 us -> none  [densify(): pl.pallas_call(dense_kernel, out_shape=(jax.ShapeDtypeStruct((width, hidd...]
    unnamed x0 -> x2, local copies, waits for them, and re-layouts: none -> 3.13 us
    another operation x1 -> x0, other arithmetic: 1.69 us -> none  [body(): mine = jnp.stack([tokens, grad_out])]
    squeeze x1 -> x0, local copies, waits for them, and re-layouts: 1.68 us -> none  [body(): return (total[0], total[1], grad_up[None], grad_down[None])]
where the time goes in v3:
time: 118 us; the launch traced here: 116 us
  Pallas kernels  109 us (92%)
  local copies, waits for them, and re-layouts  3.13 us (3%)
  other arithmetic  2.1 us (2%)
  between operations  1.29 us (1%)
    pallas_call x1, Pallas kernels, layer(): pl.pallas_call(functools.partial(layer_kernel, n_dp, n_tile), out_shape=(...  84.8 us
    pallas_call x1, Pallas kernels, grads(): pl.pallas_call(functools.partial(grads_kernel, scale), grid=(slots // gro...  24.6 us
    unnamed x2, local copies, waits for them, and re-layouts  3.13 us

profile of v3, /device:TPU:16, one launch (start us, length us, event | category | flops | bytes accessed | tf_op | source)
XLA Modules:
  0.0 115.9 jit_solution(14931908997520387017)
XLA Ops:
  1.3 0.7 pad_add_fusion.info
  1.9 0.7 compare_select_fusion
  2.7 0.7 select_reduce_fusion.slot_of
  3.4 84.8 %layer.1 = (bf16[4,8,2,128,512]{4,3,2,1,0:T(8,128)(2,1)}, bf16[4,4,2,128,512]{4,3,2,1,0:T(8,128)(2,1)}, bf16[128,512]{1,0:T(8,128)(2,1)}, bf16[128,512]{1,0:T(8,128)(2,1)}) custom-call(s32[512]{0:T(512)} %select_reduce_fusion.slot_of, bf16[128,512]{1,0:T(8,128)(2,1)} %tokens.1, bf16[128,512]{1,0:T(8,128)(2,1)} %grad_out.1, bf16[256,128,128]{2,1,0:T(8,128)(2,1)} %bitcast.10, ...), custom_call_target="tpu_custom_call" | custom-call | tf_op jit(solution)/shard_map/layer/pallas_call | solution.py:238
  88.2 24.6 %grads.1 = (f32[64,128,128]{2,1,0:T(8,128)}, f32[64,128,128]{2,1,0:T(8,128)}) custom-call(s32[256]{0:T(256)} %bitcast.13, s32[256]{0:T(256)} %bitcast.14, s32[2]{0:T(128)} %pad_add_fusion.info, bf16[4,8,2,128,512]{4,3,2,1,0:T(8,128)(2,1)} %get-tuple-element.12.x, bf16[4,4,2,128,512]{4,3,2,1,0:T(8,128)(2,1)} %get-tuple-element.13.hg), custom_call_target="tpu_custom_call" | custom-call | flops 2147483648 | bytes 20971520 | tf_op jit(solution)/shard_map/grads/pallas_call | solution.py:310
  112.8 1.6 %copy.14 = bf16[128,512]{1,0:T(8,128)(2,1)} copy(bf16[128,512]{1,0:T(8,128)(2,1)} %get-tuple-element.20) | data formatting | bytes 262144
  114.3 1.6 %copy.15 = bf16[128,512]{1,0:T(8,128)(2,1)} copy(bf16[128,512]{1,0:T(8,128)(2,1)} %get-tuple-element.21) | data formatting | bytes 262144

commit v4 on v3

--- a/solution.py
+++ b/solution.py
@@ -22,7 +22,7 @@
 TN = (((0,), (0,)), ((), ()))
 
 
-def layer_kernel(n_dp, n_tile, slot_of, tokens, grad_out, up, down, x_all, hg_all, mixed, grad_in,
+def layer_kernel(n_dp, n_tile, slot_of, tokens, grad_out, up, down, x_all, hg_all, part,
                  xz, up_t, down_t, up_v, down_v, pre, hg, outbox, inbox,
                  own_sem, z_send, z_recv, f_send, f_recv, d_send, d_recv, l_send, l_recv, e_send, e_recv,
                  h_send, h_recv, m_send, m_recv, r_send, r_recv):
@@ -84,8 +84,12 @@
         slot = hg_all.at[sources[k], p, k]
         return to(slot, slot, m_send.at[k, p], m_recv.at[k, p], targets[1 - k], me)
 
-    def r_copy(i):
-        return to(outbox.at[i], inbox.at[i], r_send.at[i], r_recv.at[i], dp, (me + i) % n_tile)
+    def s_copy(j):
+        return to(outbox.at[j], inbox.at[j], r_send.at[j], r_recv.at[j], dp, sib)
+
+    def r_copy(j):
+        i = n_z + j
+        return to(outbox.at[i], inbox.at[i], r_send.at[i], r_recv.at[i], dp, 2 * ((z + j) % n_z) + core)
 
     def landed(j):
         for k in direct:
@@ -95,8 +99,8 @@
             e_copy(k, j).start()
 
     barrier = pltpu.get_barrier_semaphore()
-    for i in range(1, n_tile):
-        pl.semaphore_signal(barrier, inc=1, device_id={"dp": dp, "tile": (me + i) % n_tile},
+    for t in [sib] + [2 * ((z + j) % n_z) + core for j in range(1, n_z)]:
+        pl.semaphore_signal(barrier, inc=1, device_id={"dp": dp, "tile": t},
                             device_id_type=pl.DeviceIdType.MESH)
     for k in direct:
         pl.semaphore_signal(barrier, inc=1, device_id={"dp": targets[k], "tile": me},
@@ -110,7 +114,7 @@
     up_t[slots] = jnp.zeros((side, side), up_t.dtype)
     down_t[slots] = jnp.zeros((side, side), down_t.dtype)
     pre[...] = jnp.zeros_like(pre)
-    pl.semaphore_wait(barrier, n_tile - 1 + len(targets))
+    pl.semaphore_wait(barrier, n_z + len(targets))
     for copy in own:
         copy.wait()
     for j in range(1, n_z):
@@ -162,24 +166,35 @@
     for copy in keep:
         copy.start()
 
-    def terms(i):
-        t = (me + i) % n_tile
+    def terms(t):
         out = jnp.zeros((pre.shape[1], feats), jnp.float32)
         back = jnp.zeros((pre.shape[1], feats), jnp.float32)
         for p in range(pieces):
             span = slice(p * piece, (p + 1) * piece)
             out += jnp.dot(hg[p, 0], down_v[t, span, :], preferred_element_type=jnp.float32)
             back += lax.dot_general(hg[p, 1], up_v[t, :, span], NT, preferred_element_type=jnp.float32)
-        outbox[i, 0] = out.astype(jnp.bfloat16)
-        outbox[i, 1] = back.astype(jnp.bfloat16)
-
-    @pl.loop(1, n_tile)
-    def _(i):
-        terms(i)
-        r_copy(i).start()
+        return out, back
+
+    @pl.loop(0, n_z)
+    def _(j):
+        out, back = terms(2 * ((z + j) % n_z) + 1 - core)
+        outbox[j, 0] = out.astype(jnp.bfloat16)
+        outbox[j, 1] = back.astype(jnp.bfloat16)
+        s_copy(j).start()
+
+    def merged(j):
+        out, back = terms(2 * ((z + j) % n_z) + core)
+        s_copy(j).wait_recv()
+        outbox[n_z + j, 0] = (out + inbox[j, 0].astype(jnp.float32)).astype(jnp.bfloat16)
+        outbox[n_z + j, 1] = (back + inbox[j, 1].astype(jnp.float32)).astype(jnp.bfloat16)
+
+    @pl.loop(1, n_z)
+    def _(j):
+        merged(j)
+        r_copy(j).start()
 
     landed(n_z - 1)
-    terms(0)
+    merged(0)
     for p in range(pieces):
         if square:
             for k in direct:
@@ -190,14 +205,13 @@
             for k in direct:
                 l_copy(k, j).wait_recv()
             e_copy(2, j).start()
-    mix = outbox[0, 0].astype(jnp.float32)
-    back = outbox[0, 1].astype(jnp.float32)
-    for i in range(1, n_tile):
-        r_copy(i).wait_recv()
-        mix = mix + inbox[i, 0].astype(jnp.float32)
-        back = back + inbox[i, 1].astype(jnp.float32)
-    mixed[...] = mix.astype(jnp.bfloat16)
-    grad_in[...] = back.astype(jnp.bfloat16)
+    for half in range(2):
+        total = outbox[n_z, half].astype(jnp.float32)
+        for j in range(1, n_z):
+            if half == 0:
+                r_copy(j).wait_recv()
+            total = total + inbox[n_z + j, half].astype(jnp.float32)
+        part[half] = total.astype(jnp.bfloat16)
     for copy in keep:
         copy.wait()
     for j in range(n_z):
@@ -217,8 +231,10 @@
                 m_copy(k, p).wait()
             else:
                 h_copy(k, p).wait_recv()
-    for i in range(1, n_tile):
-        r_copy(i).wait_send()
+    for j in range(n_z):
+        s_copy(j).wait_send()
+        if j:
+            r_copy(j).wait_send()
 
 
 def layer(slot_of, tokens, grad_out, up, down, n_dp, n_tile):
@@ -240,11 +256,10 @@
         out_shape=(
             jax.ShapeDtypeStruct((n_dp, n_tile, 2, count_tok, feats), kind),
             jax.ShapeDtypeStruct((n_dp,) + packed, kind),
-            jax.ShapeDtypeStruct(tokens.shape, kind),
-            jax.ShapeDtypeStruct(tokens.shape, kind),
+            jax.ShapeDtypeStruct((2,) + tokens.shape, kind),
         ),
         in_specs=[pl.BlockSpec(memory_space=pltpu.SMEM), hbm, hbm, hbm, hbm],
-        out_specs=(hbm, hbm, vmem, vmem),
+        out_specs=(hbm, hbm, vmem),
         scratch_shapes=[
             box,
             pltpu.VMEM((slots + 1, side, side), kind),
@@ -271,62 +286,64 @@
     )(slot_of, tokens, grad_out, up, down)
 
 
-def grads_kernel(scale, rows, cols, info, x, hg, grad_up, grad_down):
+def grads_kernel(scale, rows, cols, info, x, hg, part, grad_up, grad_down, mixed, grad_in):
     group, side = grad_up.shape[0], grad_up.shape[1]
     per = x.shape[4] // side
     wide = hg.shape[4] // side
     base = info[1] + pl.program_id(0) * group
-
-    for j in range(group):
-        s = base + j
-        live = s < info[0]
-
-        @pl.when(live)
-        def _():
-            c = cols[s]
-            owner = c // per
-            f = pl.multiple_of((c - owner * per) * side, side)
-            tokens = x.shape[0] * x.shape[3]
+    tokens = x.shape[0] * x.shape[3]
+
+    @pl.when(pl.program_id(0) == 0)
+    def _():
+        mixed[...] = part[0]
+        grad_in[...] = part[1]
+
+    @pl.when(base < info[0])
+    def _():
+        for j in range(group):
+            s = base + j
+            owner = cols[s] // per
+            f = pl.multiple_of((cols[s] - owner * per) * side, side)
+            p = rows[s] // wide
+            r = pl.multiple_of((rows[s] - p * wide) * side, side)
             xs = x[:, owner, 0, :, pl.ds(f, side)].reshape(tokens, side)
             dys = x[:, owner, 1, :, pl.ds(f, side)].reshape(tokens, side)
-            p = rows[s] // wide
-            r = pl.multiple_of((rows[s] - p * wide) * side, side)
             h = hg[:, p, 0, :, pl.ds(r, side)].reshape(tokens, side)
             g = hg[:, p, 1, :, pl.ds(r, side)].reshape(tokens, side)
-            grad_up[j] = lax.dot_general(xs, g, TN, preferred_element_type=jnp.float32) * scale
-            grad_down[j] = lax.dot_general(h, dys, TN, preferred_element_type=jnp.float32) * scale
-
-        @pl.when(jnp.logical_not(live))
-        def _():
-            grad_up[j] = jnp.zeros((side, side), jnp.float32)
-            grad_down[j] = jnp.zeros((side, side), jnp.float32)
-
-
-def grads(rows, cols, info, x, hg, slots, side, scale):
+            up_sum = lax.dot_general(xs, g, TN, preferred_element_type=jnp.float32) * scale
+            down_sum = lax.dot_general(h, dys, TN, preferred_element_type=jnp.float32) * scale
+            grad_up[j] = jnp.where(s < info[0], up_sum, 0.0)
+            grad_down[j] = jnp.where(s < info[0], down_sum, 0.0)
+
+    @pl.when(base >= info[0])
+    def _():
+        grad_up[...] = jnp.zeros_like(grad_up)
+        grad_down[...] = jnp.zeros_like(grad_down)
+
+
+def grads(rows, cols, info, x, hg, part, slots, side, scale):
     smem = pl.BlockSpec(memory_space=pltpu.SMEM)
     group = min(8, slots)
     out = pl.BlockSpec((group, side, side), lambda i: (i, 0, 0))
     shape = jax.ShapeDtypeStruct((slots, side, side), jnp.float32)
+    flat = jax.ShapeDtypeStruct(part.shape[1:], part.dtype)
+    flat_spec = pl.BlockSpec(part.shape[1:], lambda i: (0, 0))
     return pl.pallas_call(
         functools.partial(grads_kernel, scale),
         grid=(slots // group,),
-        out_shape=(shape, shape),
+        out_shape=(shape, shape, flat, flat),
         in_specs=[
             smem,
             smem,
             smem,
             pl.BlockSpec(x.shape, lambda i: (0,) * 5, pipeline_mode=pl.Buffered(1)),
             pl.BlockSpec(hg.shape, lambda i: (0,) * 5, pipeline_mode=pl.Buffered(1)),
+            pl.BlockSpec(part.shape, lambda i: (0,) * 3, pipeline_mode=pl.Buffered(1)),
         ],
-        out_specs=(out, out),
+        out_specs=(out, out, flat_spec, flat_spec),
         compiler_params=pltpu.CompilerParams(vmem_limit_bytes=VMEM_LIMIT),
-        cost_estimate=pl.CostEstimate(
-            flops=4 * slots * side * side * x.shape[0] * x.shape[3],
-            bytes_accessed=8 * slots * side * side + 2 * x.size + 2 * hg.size,
-            transcendentals=0,
-        ),
         name="grads",
-    )(rows, cols, info, x, hg)
+    )(rows, cols, info, x, hg, part)
 
 
 def body(tokens, grad_out, up_tiles, down_tiles, tile_rows, tile_cols, tile_count):
@@ -338,12 +355,14 @@
     place = jnp.where(number < tile_count[0], tile_cols[0] * high + tile_rows[0], -1)
     hit = place[None, :] == jnp.arange(cells, dtype=jnp.int32)[:, None]
     slot_of = jnp.min(jnp.where(hit, number[None, :], slots), axis=1)
-    x_all, hg_all, mixed, grad_in = layer(
+    x_all, hg_all, part = layer(
         slot_of, tokens, grad_out, up_tiles[0], down_tiles[0], n_dp, n_tile
     )
     share = slots // n_dp
     info = jnp.concatenate([tile_count, (lax.axis_index("dp") * share).astype(jnp.int32)[None]])
-    grad_up, grad_down = grads(tile_rows[0], tile_cols[0], info, x_all, hg_all, share, side, 1.0 / n_dp)
+    grad_up, grad_down, mixed, grad_in = grads(
+        tile_rows[0], tile_cols[0], info, x_all, hg_all, part, share, side, 1.0 / n_dp
+    )
     return (mixed, grad_in, grad_up[None], grad_down[None])
 
 

time: 118 us -> 105 us (0.89); the launches traced: 116 us -> 105 us
  Pallas kernels: 109 us -> 101 us
  local copies, waits for them, and re-layouts: 3.13 us -> 0 us
    pallas_call x1, Pallas kernels: 24.6 us -> 12.9 us  [grads(): pl.pallas_call(functools.partial(grads_kernel, scale), grid=(slots // gro...]
    pallas_call x1, Pallas kernels: 84.8 us -> 88.3 us  [layer(): pl.pallas_call(functools.partial(layer_kernel, n_dp, n_tile), out_shape=(...]
    unnamed x2 -> x0, local copies, waits for them, and re-layouts: 3.13 us -> none
where the time goes in v4:
time: 105 us
  Pallas kernels  101 us (96%)
  other arithmetic  2.1 us (2%)
  between operations  1.29 us (1%)
    pallas_call x1, Pallas kernels, layer(): pl.pallas_call(functools.partial(layer_kernel, n_dp, n_tile), out_shape=(...  88.3 us
    pallas_call x1, Pallas kernels, grads(): pl.pallas_call(functools.partial(grads_kernel, scale), grid=(slots // gro...  12.9 us

profile of v4, /device:TPU:16, one launch (start us, length us, event | category | flops | bytes accessed | tf_op | source)
XLA Modules:
  0.0 104.5 jit_solution(9727227672784662923)
XLA Ops:
  1.3 0.7 pad_add_fusion.info
  1.9 0.7 compare_select_fusion
  2.7 0.7 select_reduce_fusion.slot_of
  3.4 88.3 %layer.1 = (bf16[4,8,2,128,512]{4,3,2,1,0:T(8,128)(2,1)}, bf16[4,4,2,128,512]{4,3,2,1,0:T(8,128)(2,1)}, bf16[2,128,512]{2,1,0:T(8,128)(2,1)}) custom-call(s32[512]{0:T(512)} %select_reduce_fusion.slot_of, bf16[128,512]{1,0:T(8,128)(2,1)} %tokens.1, bf16[128,512]{1,0:T(8,128)(2,1)} %grad_out.1, bf16[256,128,128]{2,1,0:T(8,128)(2,1)} %bitcast.10, ...), custom_call_target="tpu_custom_call" | custom-call | tf_op jit(solution)/shard_map/layer/pallas_call | solution.py:254
  91.7 12.9 %grads.1 = (f32[64,128,128]{2,1,0:T(8,128)}, f32[64,128,128]{2,1,0:T(8,128)}, bf16[128,512]{1,0:T(8,128)(2,1)}, bf16[128,512]{1,0:T(8,128)(2,1)}) custom-call(s32[256]{0:T(256)} %bitcast.12, s32[256]{0:T(256)} %bitcast.13, s32[2]{0:T(128)} %pad_add_fusion.info, bf16[4,8,2,128,512]{4,3,2,1,0:T(8,128)(2,1)} %get-tuple-element.11.x, ...), custom_call_target="tpu_custom_call" | custom-call | tf_op jit(solution)/shard_map/grads/pallas_call | solution.py:331

commit v5 on v4

--- a/solution.py
+++ b/solution.py
@@ -125,7 +125,7 @@
     for copy in load:
         copy.wait()
 
-    def gather_in(t):
+    def fill(t):
         wide = feats // side
         high = hidden // side
 
@@ -137,12 +137,15 @@
                 up_v[t, c * side:(c + 1) * side, at] = up_t[slot]
                 down_v[t, at, c * side:(c + 1) * side] = down_t[slot]
 
+    def gather_in(t):
         @pl.loop(0, hidden // block)
         def _(b):
             at = pl.ds(pl.multiple_of(b * block, block), block)
             pre[0, :, at] += jnp.dot(xz[t, 0], up_v[t, :, at], preferred_element_type=jnp.float32)
             pre[1, :, at] += lax.dot_general(xz[t, 1], down_v[t, at, :], NT, preferred_element_type=jnp.float32)
 
+    fill(owner(0))
+    fill(other(0))
     for j in range(n_z):
         if j:
             z_copy(j).wait_recv()
@@ -150,6 +153,9 @@
             for k in direct:
                 d_copy(k, j).start()
         gather_in(owner(j))
+        if j + 1 < n_z:
+            fill(owner(j + 1))
+            fill(other(j + 1))
         f_copy(j).wait_recv()
         gather_in(other(j))
         if j:
@@ -195,16 +201,20 @@
 
     landed(n_z - 1)
     merged(0)
-    for p in range(pieces):
-        if square:
+    def crossed(j):
+        for k in direct:
+            l_copy(k, j).wait_recv()
+        e_copy(2, j).start()
+
+    if square:
+        for j in range(n_z - 1):
+            crossed(j)
+        for p in range(pieces):
             for k in direct:
                 h_copy(k, p).wait_recv()
                 m_copy(k, p).start()
-    if square:
-        for j in range(n_z):
-            for k in direct:
-                l_copy(k, j).wait_recv()
-            e_copy(2, j).start()
+            if p == pieces // 2:
+                crossed(n_z - 1)
     for half in range(2):
         total = outbox[n_z, half].astype(jnp.float32)
         for j in range(1, n_z):

time: 105 us -> 104 us (level)
  no operation moved by 1% of the time
where the time goes in v5:
time: 104 us
  Pallas kernels  100 us (96%)
  other arithmetic  2.1 us (2%)
  between operations  1.29 us (1%)
    pallas_call x1, Pallas kernels, layer(): pl.pallas_call(functools.partial(layer_kernel, n_dp, n_tile), out_shape=(...  87.4 us
    pallas_call x1, Pallas kernels, grads(): pl.pallas_call(functools.partial(grads_kernel, scale), grid=(slots // gro...  12.9 us

profile of v5, /device:TPU:16, one launch (start us, length us, event | category | flops | bytes accessed | tf_op | source)
XLA Modules:
  0.0 103.6 jit_solution(10360020152647402301)
XLA Ops:
  1.3 0.7 pad_add_fusion.info
  1.9 0.7 compare_select_fusion
  2.7 0.7 select_reduce_fusion.slot_of
  3.4 87.4 %layer.1 = (bf16[4,8,2,128,512]{4,3,2,1,0:T(8,128)(2,1)}, bf16[4,4,2,128,512]{4,3,2,1,0:T(8,128)(2,1)}, bf16[2,128,512]{2,1,0:T(8,128)(2,1)}) custom-call(s32[512]{0:T(512)} %select_reduce_fusion.slot_of, bf16[128,512]{1,0:T(8,128)(2,1)} %tokens.1, bf16[128,512]{1,0:T(8,128)(2,1)} %grad_out.1, bf16[256,128,128]{2,1,0:T(8,128)(2,1)} %bitcast.10, ...), custom_call_target="tpu_custom_call" | custom-call | tf_op jit(solution)/shard_map/layer/pallas_call | solution.py:264
  90.7 12.9 %grads.1 = (f32[64,128,128]{2,1,0:T(8,128)}, f32[64,128,128]{2,1,0:T(8,128)}, bf16[128,512]{1,0:T(8,128)(2,1)}, bf16[128,512]{1,0:T(8,128)(2,1)}) custom-call(s32[256]{0:T(256)} %bitcast.12, s32[256]{0:T(256)} %bitcast.13, s32[2]{0:T(128)} %pad_add_fusion.info, bf16[4,8,2,128,512]{4,3,2,1,0:T(8,128)(2,1)} %get-tuple-element.11.x, ...), custom_call_target="tpu_custom_call" | custom-call | tf_op jit(solution)/shard_map/grads/pallas_call | solution.py:341

commit v6 on v5

--- a/solution.py
+++ b/solution.py
@@ -194,12 +194,13 @@
         outbox[n_z + j, 0] = (out + inbox[j, 0].astype(jnp.float32)).astype(jnp.bfloat16)
         outbox[n_z + j, 1] = (back + inbox[j, 1].astype(jnp.float32)).astype(jnp.bfloat16)
 
+    landed(n_z - 1)
+
     @pl.loop(1, n_z)
     def _(j):
         merged(j)
         r_copy(j).start()
 
-    landed(n_z - 1)
     merged(0)
     def crossed(j):
         for k in direct:

time: 104 us -> 104 us (level)
  no operation moved by 1% of the time
where the time goes in v6:
time: 104 us
  Pallas kernels  100 us (96%)
  other arithmetic  2.1 us (2%)
  between operations  1.29 us (1%)
    pallas_call x1, Pallas kernels, layer(): pl.pallas_call(functools.partial(layer_kernel, n_dp, n_tile), out_shape=(...  87.4 us
    pallas_call x1, Pallas kernels, grads(): pl.pallas_call(functools.partial(grads_kernel, scale), grid=(slots // gro...  12.9 us

profile of v6, /device:TPU:16, one launch (start us, length us, event | category | flops | bytes accessed | tf_op | source)
XLA Modules:
  0.0 103.6 jit_solution(9810881739078925196)
XLA Ops:
  1.3 0.7 pad_add_fusion.info
  1.9 0.7 compare_select_fusion
  2.7 0.7 select_reduce_fusion.slot_of
  3.4 87.4 %layer.1 = (bf16[4,8,2,128,512]{4,3,2,1,0:T(8,128)(2,1)}, bf16[4,4,2,128,512]{4,3,2,1,0:T(8,128)(2,1)}, bf16[2,128,512]{2,1,0:T(8,128)(2,1)}) custom-call(s32[512]{0:T(512)} %select_reduce_fusion.slot_of, bf16[128,512]{1,0:T(8,128)(2,1)} %tokens.1, bf16[128,512]{1,0:T(8,128)(2,1)} %grad_out.1, bf16[256,128,128]{2,1,0:T(8,128)(2,1)} %bitcast.10, ...), custom_call_target="tpu_custom_call" | custom-call | tf_op jit(solution)/shard_map/layer/pallas_call | solution.py:265
  90.7 12.9 %grads.1 = (f32[64,128,128]{2,1,0:T(8,128)}, f32[64,128,128]{2,1,0:T(8,128)}, bf16[128,512]{1,0:T(8,128)(2,1)}, bf16[128,512]{1,0:T(8,128)(2,1)}) custom-call(s32[256]{0:T(256)} %bitcast.12, s32[256]{0:T(256)} %bitcast.13, s32[2]{0:T(128)} %pad_add_fusion.info, bf16[4,8,2,128,512]{4,3,2,1,0:T(8,128)(2,1)} %get-tuple-element.11.x, ...), custom_call_target="tpu_custom_call" | custom-call | tf_op jit(solution)/shard_map/grads/pallas_call | solution.py:342
